TPU v7x, 256 devices: a whole 4x4x8 slice. The times are simulated.
256 devices in a mesh: tm: 8 (over z), row: 8 (over x, core), obs: 4 (over y).
Axes of the slice: x: 4, y: 4, z: 8, core: 2. Of those that a mesh axis runs over, the one named last changes fastest.
Arguments:
- dyn_pattern: int32 [16, 8, 3], P('tm'), may hold values from 0 to 7
- dyn_values: float32 [16, 1024, 384], P('tm', ('row', 'obs')), may hold values from -0.3125 to 0.3125
- offsets: float32 [16, 1024], P('tm', ('row', 'obs')), may hold values from -6 to 6
- covariance: float32 [16, 1024, 1024], P('tm', ('row', 'obs')), may hold values from -1 to 14, as said below
- obs_block: int32 [16, 128], P('tm'), may hold values from 0 to 7
- obs_matrix: float32 [16, 128, 256], P('tm', 'obs'), may hold values from -0.375 to 0.375
- obs_data: float32 [16, 128], P('tm', 'obs'), may hold values from -6 to 6
Outputs:
- scan_dynamics: float32 [8, 1024, 1024], P('tm', ('row', 'obs'))
- scan_offset: float32 [8, 1024], P('tm', ('row', 'obs'))
- scan_covariance: float32 [8, 1024, 1024], P('tm', ('row', 'obs'))
- scan_factor: float32 [8, 1024, 512], P('tm', ('row', 'obs'))
- scan_information: float32 [8, 1024], P('tm', ('row', 'obs'))
Inputs may be any that keep to these rules, and one draw needn't show every extreme that they name: `dyn_pattern`: each entry names a block column. `obs_block`: each entry names a state block. Each covariance is symmetric and positive definite.
All inputs are finite; a program needn't handle non-finite values.
Results may differ from a plain program's by a relative error of at most 0.00019.
Values sent between devices are 32-bit elements; how exact they have to be, the bound alone decides.
A program may use at most 128 MiB of HBM per device.

v0:
```python
import jax
import jax.numpy as jnp
from jax import lax
from jax.sharding import PartitionSpec as P

largest_value = lax.Precision.HIGHEST


def shifted(block, axis, distance):
    devices = range(lax.axis_size(axis))
    route = [(i - distance, i) for i in devices if i - distance in devices]
    return lax.ppermute(block, axis, route)


def product(left, right):
    return jnp.dot(left, right, precision=largest_value, preferred_element_type=jnp.float32)


def lower_solve(lower, rhs):
    return lax.linalg.triangular_solve(lower, rhs, left_side=True, lower=True)


def assemble_dynamics(pattern, values):
    number_of_blocks = pattern.shape[0]
    per_row = pattern.shape[1]
    states = values.shape[0]
    block_extent = states // number_of_blocks
    indicator_matrix = (
        pattern[:, :, None] == jnp.arange(number_of_blocks, dtype=jnp.int32)[None, None, :]
    ).astype(jnp.float32)
    blocks = values.reshape(number_of_blocks, block_extent, per_row, block_extent)
    return jnp.einsum("ckd,cikj->cidj", indicator_matrix, blocks, precision=largest_value).reshape(
        states, states
    )


def assemble_factor(indices, matrix, number_of_blocks):
    item_count = matrix.shape[0]
    block_extent = matrix.shape[1] // 2
    reach = (indices[:, None] + jnp.arange(2, dtype=jnp.int32)[None, :]) % number_of_blocks
    indicator_matrix = (
        reach[:, :, None] == jnp.arange(number_of_blocks, dtype=jnp.int32)[None, None, :]
    ).astype(jnp.float32)
    piece_list = matrix.reshape(item_count, 2, block_extent)
    return jnp.einsum(
        "onr,onz->rzo", indicator_matrix, piece_list, precision=largest_value
    ).reshape(number_of_blocks * block_extent, item_count)


def combine(
    prior_dyn,
    prior_offsets,
    prior_cov,
    prior_factor,
    prior_zeta,
    own_dyn,
    own_offsets,
    own_cov,
    own_factor,
    own_zeta,
    row_start,
):
    panel_rows = prior_cov.shape[0]
    rank_width = own_factor.shape[1]
    own_pan = lax.dynamic_slice_in_dim(own_dyn, row_start, panel_rows, 0)
    gain_pan = product(prior_cov, own_factor)
    gain_rows = lax.all_gather(gain_pan, ("row", "obs"), axis=0, tiled=True)
    identity = jnp.eye(rank_width, dtype=jnp.float32)
    factor_pan = lax.dynamic_slice_in_dim(own_factor, row_start, panel_rows, 0)
    system = identity + lax.psum(product(factor_pan.T, gain_pan), ("row", "obs"))
    lower = jnp.linalg.cholesky(system)
    carried = product(own_dyn, gain_rows)
    observed = product(prior_dyn.T, own_factor)
    upper_part = lower_solve(lower, observed.T)
    weights = lower_solve(lower, carried.T).T
    weight_pan = lax.dynamic_slice_in_dim(weights, row_start, panel_rows, 0)
    spread_pan = product(prior_cov, own_dyn.T)
    moved = product(own_pan, lax.all_gather(spread_pan, ("row", "obs"), axis=0, tiled=True))
    new_dyn = product(own_pan, prior_dyn) - product(weight_pan, upper_part)
    new_cov = moved - product(weight_pan, weights.T) + own_cov
    residual = own_zeta - product(own_factor.T, prior_offsets)
    solved = lower_solve(lower, residual[:, None])[:, 0]
    new_offsets = product(own_pan, prior_offsets) + product(weight_pan, solved) + own_offsets
    upper_pan = lax.dynamic_slice_in_dim(upper_part, row_start, panel_rows, 1).T
    new_factor = jnp.concatenate([upper_pan, prior_factor], axis=1)
    new_zeta = jnp.concatenate([solved, prior_zeta])
    return (new_dyn, new_offsets, new_cov, new_factor, new_zeta)


def per_device(dyn_pattern, dyn_values, offsets, covariance, obs_block, obs_matrix, obs_data):
    panel_rows = covariance.shape[1]
    row_start = lax.axis_index(("row", "obs")) * panel_rows
    number_of_blocks = dyn_pattern.shape[1]
    obs_rows, obs_values = (
        lax.all_gather(obs_matrix, "obs", axis=1, tiled=True),
        lax.all_gather(obs_data, "obs", axis=1, tiled=True),
    )
    row_values, row_offsets = (
        lax.all_gather(dyn_values, ("row", "obs"), axis=1, tiled=True),
        lax.all_gather(offsets, ("row", "obs"), axis=1, tiled=True),
    )
    first_dyn = assemble_dynamics(dyn_pattern[0], row_values[0])
    second_dyn = assemble_dynamics(dyn_pattern[1], row_values[1])
    first_factor = assemble_factor(obs_block[0], obs_rows[0], number_of_blocks)
    second_factor = assemble_factor(obs_block[1], obs_rows[1], number_of_blocks)
    first_pan = lax.dynamic_slice_in_dim(first_factor, row_start, panel_rows, 0)
    dyn_pan, off_pan, cov_pan, fac_pan, zeta_full = combine(
        first_dyn,
        row_offsets[0],
        covariance[0],
        first_pan,
        obs_values[0],
        second_dyn,
        offsets[1],
        covariance[1],
        second_factor,
        obs_values[1],
        row_start,
    )
    later_pan, later_cov, later_off, later_fac, later_zeta = shifted(
        (dyn_pan, cov_pan, off_pan, fac_pan, zeta_full), "tm", -1
    )
    prior_full, later_full, later_factor, prior_offsets = (
        lax.all_gather(dyn_pan, ("row", "obs"), axis=0, tiled=True),
        lax.all_gather(later_pan, ("row", "obs"), axis=0, tiled=True),
        lax.all_gather(later_fac, ("row", "obs"), axis=0, tiled=True),
        lax.all_gather(off_pan, ("row", "obs"), axis=0, tiled=True),
    )
    top_dyn, top_off, top_cov, top_fac, top_zeta = combine(
        prior_full,
        prior_offsets,
        cov_pan,
        fac_pan,
        zeta_full,
        later_full,
        later_off,
        later_cov,
        later_factor,
        later_zeta,
        row_start,
    )
    even_turn = lax.axis_index("tm") % 2 == 0
    padded_fac = jnp.concatenate([fac_pan, jnp.zeros_like(fac_pan)], axis=1)
    padded_zeta = jnp.concatenate([zeta_full, jnp.zeros_like(zeta_full)])
    out_dyn = jnp.where(even_turn, top_dyn, dyn_pan)
    out_off = jnp.where(even_turn, top_off, off_pan)
    out_cov = jnp.where(even_turn, top_cov, cov_pan)
    out_fac = jnp.where(even_turn, top_fac, padded_fac)
    out_zeta = jnp.where(even_turn, top_zeta, padded_zeta)
    output_information = product(out_fac, out_zeta)
    return (out_dyn[None], out_off[None], out_cov[None], out_fac[None], output_information[None])


def solution(mesh):
    placed = (
        P("tm", None, None),
        P("tm", ("row", "obs"), None),
        P("tm", ("row", "obs")),
        P("tm", ("row", "obs"), None),
        P("tm", None),
        P("tm", "obs", None),
        P("tm", "obs"),
    )
    return jax.shard_map(
        per_device,
        mesh=mesh,
        in_specs=placed,
        out_specs=(
            P("tm", ("row", "obs"), None),
            P("tm", ("row", "obs")),
            P("tm", ("row", "obs"), None),
            P("tm", ("row", "obs"), None),
            P("tm", ("row", "obs")),
        ),
        check_vma=False,
    )
```

profile of v0, /device:TPU:1, one launch (start us, length us, event | category | flops | bytes accessed | tf_op | source)
XLA Modules:
  0.0 616.6 jit_solution(8064863237237655006)
XLA Ops:
  7.2 0.7 all-gather.10.cloned.1.call-update
  8.0 11.5 %all_gather.37 = f32[2,128,256]{2,1,0:T(8,128)S(1)} all-gather(f32[2,32,256]{2,1,0:T(8,128)} %param.16), channel_id=1, replica_groups=mesh['tm'=8,'row'=8,'obs'=4] {'obs'}, dimensions={1}, use_global_device_ids=true | all-gather | bytes 327680 | tf_op jit(solution)/shard_map/all_gather | solution.py:95
  19.5 0.8 slice_bitcast_fusion.12
  20.4 0.9 fusion.36
  21.4 1.5 fusion.42
  23.0 0.9 fusion.83
  24.0 40.9 %all-gather.10.cloned.1.call-done = f32[2,1024,384]{2,1,0:T(8,128)} async-done(((f32[2,32,384]{2,1,0:T(8,128)}), f32[2,1024,384]{2,1,0:T(8,128)}) %all-gather.10.cloned.1.call-update) | async-done | bytes 3145744 | tf_op jit(solution)/shard_map/all_gather | solution.py:99
  64.9 3.2 fusion.135
  68.2 3.6 reshape.312
  71.8 4.3 fusion.104
  76.1 2.0 copy-done
  78.1 4.9 convolution_bitcast_fusion.1
  83.5 0.9 convolution_bitcast_fusion
  84.7 89.2 %all-reduce.5.cloned.1.call-done = f32[128,128]{1,0:T(8,128)} async-done(((f32[128,128]{1,0:T(8,128)}), f32[128,128]{1,0:T(8,128)}) %all-reduce.5.cloned.1.call-update) | async-done | bytes 65552 | tf_op jit(solution)/shard_map/psum | solution.py:70
  173.8 0.9 convert_add_fusion.1
  174.8 0.9 fusion.77
  175.6 11.7 %cholesky.60 = f32[128,128]{1,0:T(8,128)S(1)} custom-call(f32[128,128]{1,0:T(8,128)S(1)} %fusion.77), custom_call_target="Cholesky" | custom-call | tf_op jit(solution)/shard_map/jit(cholesky)/cholesky | solution.py:71
  188.0 0.7 fusion.55
  188.7 9.8 %custom-call.31 = f32[1,128,128]{1,2,0:T(8,128)S(1)} custom-call(f32[1,128,128]{2,1,0:T(8,128)S(1)} %fusion.55), custom_call_target="InvertDiagBlocksLowerTriangular" | custom-call | tf_op jit(solution)/shard_map/triangular_solve/custom-call.4 | solution.py:20
  198.5 2.2 reshape.313
  200.7 4.3 fusion.107
  205.1 2.0 copy-done.2
  207.1 3.0 fusion
  210.9 1.3 collective-permute-start.1
  212.1 3.8 collective-permute-done.1
  216.6 42.6 %all_gather.38 = f32[1024,128]{1,0:T(8,128)S(1)} all-gather(f32[32,128]{1,0:T(8,128)S(1)} %bitcast.273), channel_id=1, replica_groups=mesh['tm'=8,'row'=8,'obs'=4] {'row','obs'}, dimensions={0}, use_global_device_ids=true | all-gather | bytes 540672 | tf_op jit(solution)/shard_map/all_gather | solution.py:67
  259.2 3.4 copy.79
  262.6 4.8 fusion.133
  268.5 3.0 fusion.6
  271.5 1.4 collective-permute-start
  273.0 4.4 collective-permute-done
  277.4 0.7 copy-done.12
  278.9 4.8 fusion.52
  284.2 1.9 fusion.138
  286.1 1.9 fusion.100
  288.1 0.7 all-gather.20.cloned.1.call-update
  288.9 40.2 %all-gather = f32[32,32,2]{1,2,0:T(2,128)S(1)} all-gather(f32[1,32,2]{1,2,0:T(2,128)S(1)} %bitcast.282), channel_id=1, replica_groups=mesh['tm'=8,'row'=8,'obs'=4] {'row','obs'}, dimensions={0}, use_global_device_ids=true | all-gather | bytes 8448 | tf_op jit(solution)/shard_map/all_gather | solution.py:100
  329.1 5.2 all-gather.1
  334.5 0.7 fusion.175
  335.7 6.7 %fusion.141 = f32[32,1024]{1,0:T(8,128)} fusion(f32[32,1024]{1,0:T(8,128)S(1)} %fusion.12, f32[1024,1024]{1,0:T(8,128)} %all-gather.12.cloned.1.call-done), kind=kOutput, calls=%fused_computation.205 | convolution fusion | flops 402653184 | bytes 4456448 | tf_op jit(solution)/shard_map/dot_general | solution.py:16
  343.9 1.3 collective-permute-start.2
  345.3 1.1 convolution_bitcast_fusion.9
  346.6 1.3 collective-permute-start.3
  348.2 63.2 %all-reduce.1 = f32[1024]{0:T(1024)S(1)} all-reduce(f32[1024]{0:T(1024)S(1)} %dynamic-update-slice.17), channel_id=1, replica_groups=mesh['tm'=8,'row'=8,'obs'=4] {'row','obs'}, use_global_device_ids=true, to_apply=%add.1 | all-reduce | flops 1024 | bytes 8192
  412.1 1.3 collective-permute-start.4
  413.4 6.0 fusion.140
  419.4 80.5 %all-reduce.7.cloned.1.call-done = f32[256,256]{0,1:T(8,128)} async-done(((f32[256,256]{0,1:T(8,128)}), f32[256,256]{0,1:T(8,128)}) %all-reduce.7.cloned.1.call-update) | async-done | bytes 262160 | tf_op jit(solution)/shard_map/psum | solution.py:70
  499.9 1.0 convert_add_fusion
  501.0 1.0 fusion.34
  502.0 11.7 %cholesky.115 = f32[128,128]{1,0:T(8,128)S(1)} custom-call(f32[128,128]{1,0:T(8,128)S(1)} %cholesky.141), custom_call_target="Cholesky" | custom-call | tf_op jit(solution)/shard_map/jit(cholesky)/cholesky | solution.py:71
  513.8 9.8 %custom-call.26 = f32[1,128,128]{1,2,0:T(8,128)S(1)} custom-call(f32[1,128,128]{2,1,0:T(8,128)S(1)} %get-tuple-element.62), custom_call_target="InvertDiagBlocksLowerTriangular" | custom-call | tf_op jit(solution)/shard_map/jit(cholesky)/cholesky | solution.py:71
  524.1 11.7 %cholesky.128 = f32[128,128]{1,0:T(8,128)S(1)} custom-call(f32[128,128]{1,0:T(8,128)S(1)} %convolution_subtract_fusion.3), custom_call_target="Cholesky" | custom-call | tf_op jit(solution)/shard_map/jit(cholesky)/cholesky | solution.py:71
  538.5 4.0 while.5
  539.1 1.4 bitcast_dynamic-update-slice_fusion.2
  541.1 1.4 bitcast_dynamic-update-slice_fusion.2
  542.5 19.8 %custom-call.33 = f32[2,128,128]{1,2,0:T(8,128)S(1)} custom-call(f32[2,128,128]{2,1,0:T(8,128)S(1)} %get-tuple-element.29), custom_call_target="InvertDiagBlocksLowerTriangular" | custom-call | tf_op jit(solution)/shard_map/triangular_solve/custom-call.5 | solution.py:20
  565.1 0.7 fusion.60
  566.5 9.2 %fusion.139 = f32[256,1024]{1,0:T(8,128)S(1)} fusion(f32[1024,256]{1,0:T(8,128)} %all-gather.20.cloned.1.call-done, f32[1024,1024]{1,0:T(8,128)} %all-gather.12.cloned.1.call-done), kind=kOutput, calls=%fused_computation.203 | convolution fusion | flops 3221225472 | bytes 6291456 | tf_op jit(solution)/shard_map/dot_general | solution.py:16
  577.7 0.7 fusion.24
  578.4 0.7 fusion.23
  579.2 4.1 fusion.14
  583.4 1.7 fusion.20
  585.1 19.4 %all-gather.22.cloned.1.call-done = f32[1024,1024]{1,0:T(8,128)} async-done(((f32[32,1024]{1,0:T(8,128)}), f32[1024,1024]{1,0:T(8,128)}) %all-gather.22.cloned.1.call-update) | async-done | bytes 4194320 | tf_op jit(solution)/shard_map/all_gather | solution.py:78
  604.5 5.4 fusion.11
  (127 shorter events, 17.6 us)
Async XLA Ops:
  7.2 16.8 %copy-start.15 = (s32[2,8,3]{1,0,2:T(2,128)S(1)}, s32[2,8,3]{1,0,2:T(2,128)}, u32[]{:S(2)}) copy-start(s32[2,8,3]{1,0,2:T(2,128)} %param.11) | copy-start | bytes 580
  7.2 57.8 %all-gather.10.cloned.1.call-start = ((), (), s32[]{:S(2)}) async-start(), calls=%async_computation | async-start | bytes 3244032 | tf_op jit(solution)/shard_map/all_gather | solution.py:99
  7.9 165.9 %all-reduce.5.cloned.1.call-start = ((), (), s32[]{:S(2)}) async-start(), calls=%async_computation.1 | async-start | bytes 131072 | tf_op jit(solution)/shard_map/psum | solution.py:70
  23.9 255.0 %all-gather.18.cloned.1.call-start = ((), (), s32[]{:S(2)}) async-start(), calls=%async_computation.5 | async-start | bytes 4325376 | tf_op jit(solution)/shard_map/all_gather | solution.py:78
  68.2 9.9 %copy-start.10 = (f32[2,32,1024]{2,1,0:T(8,128)S(1)}, f32[2,32,1024]{2,1,0:T(8,128)}, u32[]{:S(2)}) copy-start(f32[2,32,1024]{2,1,0:T(8,128)} %param.14) | copy-start | bytes 786436
  76.1 2.0 copy-start
  83.0 201.2 %all-gather.16.cloned.1.call-start = ((), (), s32[]{:S(2)}) async-start(), calls=%async_computation.4 | async-start | bytes 1081344 | tf_op jit(solution)/shard_map/all_gather | solution.py:126
  84.6 120.4 %copy-start.9 = (f32[8,128,128]{2,1,0:T(8,128)}, f32[8,128,128]{2,1,0:T(8,128)S(1)}, u32[]{:S(2)}) copy-start(f32[8,128,128]{2,1,0:T(8,128)S(1)} %copy.56) | copy-start | bytes 1572868
  205.0 2.0 copy-start.2
  210.9 5.0 collective-permute-start.1
  215.9 0.6 copy-start.13
  216.5 119.2 %all-gather.12.cloned.1.call-start = ((), (), s32[]{:S(2)}) async-start(), calls=%async_computation.2 | async-start | bytes 4325376 | tf_op jit(solution)/shard_map/all_gather | solution.py:125
  259.2 3.5 copy-start.1
  262.6 5.9 copy-start.6
  262.6 5.9 copy-start.3
  271.5 6.6 %copy-start.7 = (f32[32,1024]{1,0:T(8,128)}, f32[32,1024]{1,0:T(8,128)S(1)}, u32[]{:S(2)}) copy-start(f32[32,1024]{1,0:T(8,128)S(1)} %fusion.6) | copy-start | bytes 393220
  271.5 17.3 %copy-start.14 = (f32[2,32]{1,0:T(2,128)S(1)}, f32[2,32]{1,0:T(2,128)}, u32[]{:S(2)}) copy-start(f32[2,32]{1,0:T(2,128)} %param.13) | copy-start | bytes 772
  271.5 57.6 %copy-start.16 = (f32[2,32]{1,0:T(2,128)S(1)}, f32[2,32]{1,0:T(2,128)}, u32[]{:S(2)}) copy-start(f32[2,32]{1,0:T(2,128)} %param.17) | copy-start | bytes 772
  271.5 5.8 collective-permute-start
  277.4 0.7 copy-start.12
  278.1 135.3 %all-gather.14.cloned.1.call-start = ((), (), s32[]{:S(2)}) async-start(), calls=%async_computation.3 | async-start | bytes 4325376 | tf_op jit(solution)/shard_map/all_gather | solution.py:124
  278.6 221.2 %all-reduce.7.cloned.1.call-start = ((), (), s32[]{:S(2)}) async-start(), calls=%async_computation.6 | async-start | bytes 524288 | tf_op jit(solution)/shard_map/psum | solution.py:70
  283.7 58.8 %copy-start.17 = (u32[256]{0:T(256)S(1)}, u32[256]{0:T(256)}, u32[]{:S(2)}) copy-start(u32[256]{0:T(256)} %constant.217) | copy-start | bytes 3076
  284.2 127.2 %copy-start.5 = (f32[1024,256]{1,0:T(8,128)S(1)}, f32[1024,256]{1,0:T(8,128)}, u32[]{:S(2)}) copy-start(f32[1024,256]{1,0:T(8,128)} %all-gather.16.cloned.1.call-done) | copy-start | bytes 3145732
  286.1 2.0 copy-start.11
  288.1 278.4 %all-gather.20.cloned.1.call-start = ((), (), s32[]{:S(2)}) async-start(), calls=%async_computation.7 | async-start | bytes 1081344 | tf_op jit(solution)/shard_map/all_gather | solution.py:67
  288.8 315.7 %all-gather.22.cloned.1.call-start = ((), (), s32[]{:S(2)}) async-start(), calls=%async_computation.8 | async-start | bytes 4325376 | tf_op jit(solution)/shard_map/all_gather | solution.py:78
  343.9 68.2 %collective-permute-start.2 = (f32[256]{0:T(256)S(1)}, f32[256]{0:T(256)S(1)}, u32[]{:S(2)}, u32[]{:S(2)}) collective-permute-start(f32[256]{0:T(256)S(1)} %pad_maximum_fusion.5), channel_id=1, source_target_pairs={{32,0},{64,32},{96,64},{128,96},{160,128},{192,160},{224,192},{33,... | collective-permute-start | bytes 3080 | tf_op jit(solution)/shard_map/ppermute | solution.py:12
  346.6 236.8 %collective-permute-start.3 = (f32[32]{0:T(128)S(1)}, f32[32]{0:T(128)S(1)}, u32[]{:S(2)}, u32[]{:S(2)}) collective-permute-start(f32[32]{0:T(128)S(1)} %fusion.16), channel_id=1, source_target_pairs={{32,0},{64,32},{96,64},{128,96},{160,128},{192,160},{224,192},{33,... | collective-permute-start | bytes 392 | tf_op jit(solution)/shard_map/ppermute | solution.py:12
  412.1 173.0 %collective-permute-start.4 = (f32[32,1024]{1,0:T(8,128)S(1)}, f32[32,1024]{1,0:T(8,128)S(1)}, u32[]{:S(2)}, u32[]{:S(2)}) collective-permute-start(f32[32,1024]{1,0:T(8,128)S(1)} %fusion.12), channel_id=1, source_target_pairs={{32,0},{64,32},{96,64},{128,96},{160,128},{192,160},{224,192},{33,... | collective-permute-start | bytes 393224 | tf_op jit(solution)/shard_map/ppermute | solution.py:12
  575.7 3.5 copy-start.4
  575.7 3.5 copy-start.8
Sparse Core Ops, SparseCore 0:
  10.6 54.3 all-gather.9
  68.8 104.9 all-reduce.4
  177.3 50.7 all-gather.17
  231.4 47.2 all-gather.15
  281.4 50.4 all-gather.11
  335.2 50.5 all-gather.13
  389.4 110.4 all-reduce.6
  503.0 48.6 all-gather.19
  554.3 50.1 all-gather.21
where the time goes:
time: 624 us; the launch traced here: 617 us
  waiting for transfers between devices  240 us (38%)
  blocking collectives  163 us (26%)
  other arithmetic  82 us (13%)
  matrix products  81.8 us (13%)
  local copies, waits for them, and re-layouts  25.7 us (4%)
  between operations  16.7 us (3%)
  starting transfers between devices  7.45 us (1%)
    psum x2, waiting for transfers between devices, combine(): lax.psum(product(factor_pan.T, gain_pan), ('row', 'obs'))  170 us
    dot_general x25, matrix products, product(): jnp.dot(left, right, precision=largest_value, preferred_element_type=jnp....  65.3 us
    unnamed x1, blocking collectives  63.2 us
    another operation x10, other arithmetic, combine(): lower = jnp.linalg.cholesky(system)  47 us
    all_gather x1, blocking collectives, combine(): gain_rows = lax.all_gather(gain_pan, ('row', 'obs'), axis=0, tiled=True)  42.6 us
    all_gather x1, waiting for transfers between devices, per_device(): lax.all_gather(dyn_values, ('row', 'obs'), axis=1, tiled=True)  40.9 us
    all_gather x1, blocking collectives, per_device(): lax.all_gather(offsets, ('row', 'obs'), axis=1, tiled=True)  40.2 us
    another operation x8, other arithmetic, lower_solve(): return lax.linalg.triangular_solve(lower, rhs, left_side=True, lower=True)  30.5 us
  transfers between devices with their start and end apart: 14, of which 6 were waited for; matrix products, arithmetic and copies ran while one was open for 29% of the time, Pallas kernels for 0%

commit v1 on v0

--- a/solution.py
+++ b/solution.py
@@ -67,7 +67,7 @@
     gain_rows = lax.all_gather(gain_pan, ("row", "obs"), axis=0, tiled=True)
     identity = jnp.eye(rank_width, dtype=jnp.float32)
     factor_pan = lax.dynamic_slice_in_dim(own_factor, row_start, panel_rows, 0)
-    system = identity + lax.psum(product(factor_pan.T, gain_pan), ("row", "obs"))
+    system = identity + lax.psum(lax.psum(product(factor_pan.T, gain_pan), "obs"), "row")
     lower = jnp.linalg.cholesky(system)
     carried = product(own_dyn, gain_rows)
     observed = product(prior_dyn.T, own_factor)

time: 624 us -> 538 us (0.86)
  the two profiles are of different devices: /device:TPU:1 before, /device:TPU:224 now
where the time goes in v1:
time: 538 us; the launch traced here: 530 us
  blocking collectives  168 us (31%)
  waiting for transfers between devices  132 us (25%)
  matrix products  83.9 us (16%)
  other arithmetic  82.1 us (15%)
  local copies, waits for them, and re-layouts  27.2 us (5%)
  starting transfers between devices  18.5 us (3%)
  between operations  18.5 us (3%)
    psum x2, waiting for transfers between devices, combine(): lax.psum(product(factor_pan.T, gain_pan), 'obs')  77.9 us
    dot_general x25, matrix products, product(): jnp.dot(left, right, precision=largest_value, preferred_element_type=jnp....  67.4 us
    unnamed x1, blocking collectives  64.2 us
    another operation x10, other arithmetic, combine(): lower = jnp.linalg.cholesky(system)  47 us
    all_gather x1, blocking collectives, combine(): gain_rows = lax.all_gather(gain_pan, ('row', 'obs'), axis=0, tiled=True)  45.6 us
    psum x2, waiting for transfers between devices, combine(): lax.psum(lax.psum(product(factor_pan.T, gain_pan), 'obs'), 'row')  41.5 us
    all_gather x1, blocking collectives, per_device(): lax.all_gather(offsets, ('row', 'obs'), axis=1, tiled=True)  37.1 us
    another operation x8, other arithmetic, lower_solve(): return lax.linalg.triangular_solve(lower, rhs, left_side=True, lower=True)  30.5 us
  transfers between devices with their start and end apart: 16, of which 6 were waited for; matrix products, arithmetic and copies ran while one was open for 33% of the time, Pallas kernels for 0%

profile of v1, /device:TPU:224, one launch (start us, length us, event | category | flops | bytes accessed | tf_op | source)
XLA Modules:
  0.0 530.4 jit_solution(13532728122809845748)
XLA Ops:
  8.1 0.8 slice_bitcast_fusion.12
  8.8 13.0 %all_gather.37 = f32[2,128,256]{2,1,0:T(8,128)S(1)} all-gather(f32[2,32,256]{2,1,0:T(8,128)} %param.16), channel_id=1, replica_groups=mesh['tm'=8,'row'=8,'obs'=4] {'obs'}, dimensions={1}, use_global_device_ids=true | all-gather | bytes 327680 | tf_op jit(solution)/shard_map/all_gather | solution.py:95
  22.0 0.9 fusion.36
  23.1 1.5 fusion.42
  24.6 0.9 fusion.83
  26.2 45.4 %all-reduce.7.cloned.1.call-done = f32[128,128]{1,0:T(8,128)} async-done(((f32[128,128]{1,0:T(8,128)}), f32[128,128]{1,0:T(8,128)}) %all-reduce.7.cloned.1.call-update) | async-done | bytes 65552 | tf_op jit(solution)/shard_map/psum | solution.py:70
  71.7 6.9 %all-gather.10.cloned.1.call-done = f32[2,1024,384]{2,1,0:T(8,128)} async-done(((f32[2,32,384]{2,1,0:T(8,128)}), f32[2,1024,384]{2,1,0:T(8,128)}) %all-gather.10.cloned.1.call-update) | async-done | bytes 3145744 | tf_op jit(solution)/shard_map/all_gather | solution.py:99
  78.6 3.2 fusion.135
  81.8 3.6 reshape.312
  85.4 4.3 fusion.104
  89.7 2.0 copy-done
  91.7 4.9 convolution_bitcast_fusion.1
  97.1 0.9 convolution_bitcast_fusion
  98.3 41.5 %all-reduce.9.cloned.1.call-done = f32[128,128]{1,0:T(8,128)} async-done(((f32[128,128]{1,0:T(8,128)}), f32[128,128]{1,0:T(8,128)}) %all-reduce.9.cloned.1.call-update) | async-done | bytes 65552 | tf_op jit(solution)/shard_map/psum | solution.py:70
  139.7 0.9 convert_add_fusion.1
  140.7 0.9 fusion.77
  141.5 11.7 %cholesky.60 = f32[128,128]{1,0:T(8,128)S(1)} custom-call(f32[128,128]{1,0:T(8,128)S(1)} %fusion.77), custom_call_target="Cholesky" | custom-call | tf_op jit(solution)/shard_map/jit(cholesky)/cholesky | solution.py:71
  153.9 0.7 fusion.55
  154.6 9.8 %custom-call.31 = f32[1,128,128]{1,2,0:T(8,128)S(1)} custom-call(f32[1,128,128]{2,1,0:T(8,128)S(1)} %fusion.55), custom_call_target="InvertDiagBlocksLowerTriangular" | custom-call | tf_op jit(solution)/shard_map/triangular_solve/custom-call.4 | solution.py:20
  164.4 2.0 reshape.313
  166.4 4.3 fusion.107
  170.7 1.9 copy-done.2
  172.6 3.0 fusion
  176.4 3.3 collective-permute-start.1
  179.7 1.6 collective-permute-done.1
  181.9 45.6 %all_gather.38 = f32[1024,128]{1,0:T(8,128)S(1)} all-gather(f32[32,128]{1,0:T(8,128)S(1)} %bitcast.273), channel_id=1, replica_groups=mesh['tm'=8,'row'=8,'obs'=4] {'row','obs'}, dimensions={0}, use_global_device_ids=true | all-gather | bytes 540672 | tf_op jit(solution)/shard_map/all_gather | solution.py:67
  227.5 5.4 %copy.79 = f32[128,8,8,128]{3,1,2,0:T(8,128)} copy(f32[128,8,8,128]{3,2,1,0:T(8,128)} %bitcast.259) | data formatting | bytes 8388608
  232.9 4.8 fusion.133
  238.8 4.8 fusion.52
  244.1 1.8 fusion.138
  245.9 1.9 fusion.100
  248.1 5.2 fusion.6
  253.3 4.5 collective-permute-start
  257.8 2.5 collective-permute-done
  260.3 0.7 copy-done.10
  261.0 0.7 all-gather.14.cloned.1.call-update
  261.8 32.5 %all-reduce.11.cloned.1.call-done = f32[256,256]{0,1:T(8,128)} async-done(((f32[256,256]{0,1:T(8,128)}), f32[256,256]{0,1:T(8,128)}) %all-reduce.11.cloned.1.call-update) | async-done | bytes 262160 | tf_op jit(solution)/shard_map/psum | solution.py:70
  294.3 0.7 all-gather.20.cloned.1.call-update
  295.1 37.1 %all-gather = f32[32,32,2]{1,2,0:T(2,128)S(1)} all-gather(f32[1,32,2]{1,2,0:T(2,128)S(1)} %bitcast.282), channel_id=1, replica_groups=mesh['tm'=8,'row'=8,'obs'=4] {'row','obs'}, dimensions={0}, use_global_device_ids=true | all-gather | bytes 8448 | tf_op jit(solution)/shard_map/all_gather | solution.py:100
  332.3 7.9 %all-gather.1 = f32[4,32,2]{1,2,0:T(2,128)S(1)} all-gather(f32[1,32,2]{1,2,0:T(2,128)S(1)} %bitcast.288), channel_id=1, replica_groups=mesh['tm'=8,'row'=8,'obs'=4] {'obs'}, dimensions={0}, use_global_device_ids=true | all-gather | bytes 1280 | tf_op jit(solution)/shard_map/all_gather | solution.py:96
  340.3 0.7 fusion.175
  341.5 6.7 %fusion.141 = f32[32,1024]{1,0:T(8,128)} fusion(f32[32,1024]{1,0:T(8,128)S(1)} %fusion.12, f32[1024,1024]{1,0:T(8,128)} %all-gather.12.cloned.1.call-done), kind=kOutput, calls=%fused_computation.205 | convolution fusion | flops 402653184 | bytes 4456448 | tf_op jit(solution)/shard_map/dot_general | solution.py:16
  349.7 3.3 collective-permute-start.2
  353.0 1.1 convolution_bitcast_fusion.9
  354.4 3.3 collective-permute-start.3
  358.0 64.2 %all-reduce.1 = f32[1024]{0:T(1024)S(1)} all-reduce(f32[1024]{0:T(1024)S(1)} %dynamic-update-slice.17), channel_id=1, replica_groups=mesh['tm'=8,'row'=8,'obs'=4] {'row','obs'}, use_global_device_ids=true, to_apply=%add.1 | all-reduce | flops 1024 | bytes 8192
  422.8 3.3 collective-permute-start.4
  426.2 5.8 %fusion.140 = f32[256,1024]{1,0:T(8,128)S(1)} fusion(f32[1024,256]{1,0:T(8,128)S(1)} %copy-done.4, f32[1024,1024]{1,0:T(8,128)} %all-gather.14.cloned.1.call-done), kind=kOutput, calls=%fused_computation.204 | convolution fusion | flops 3221225472 | bytes 6291456 | tf_op jit(solution)/shard_map/dot_general | solution.py:16
  432.0 1.0 convert_add_fusion
  433.1 1.0 fusion.34
  434.1 11.7 %cholesky.115 = f32[128,128]{1,0:T(8,128)S(1)} custom-call(f32[128,128]{1,0:T(8,128)S(1)} %cholesky.141), custom_call_target="Cholesky" | custom-call | tf_op jit(solution)/shard_map/jit(cholesky)/cholesky | solution.py:71
  445.9 9.8 %custom-call.26 = f32[1,128,128]{1,2,0:T(8,128)S(1)} custom-call(f32[1,128,128]{2,1,0:T(8,128)S(1)} %get-tuple-element.62), custom_call_target="InvertDiagBlocksLowerTriangular" | custom-call | tf_op jit(solution)/shard_map/jit(cholesky)/cholesky | solution.py:71
  456.2 11.7 %cholesky.128 = f32[128,128]{1,0:T(8,128)S(1)} custom-call(f32[128,128]{1,0:T(8,128)S(1)} %convolution_subtract_fusion.3), custom_call_target="Cholesky" | custom-call | tf_op jit(solution)/shard_map/jit(cholesky)/cholesky | solution.py:71
  470.6 4.0 while.5
  471.2 1.4 bitcast_dynamic-update-slice_fusion.2
  473.2 1.4 bitcast_dynamic-update-slice_fusion.2
  474.6 19.9 %custom-call.33 = f32[2,128,128]{1,2,0:T(8,128)S(1)} custom-call(f32[2,128,128]{2,1,0:T(8,128)S(1)} %get-tuple-element.29), custom_call_target="InvertDiagBlocksLowerTriangular" | custom-call | tf_op jit(solution)/shard_map/triangular_solve/custom-call.5 | solution.py:20
  497.3 0.7 fusion.60
  498.6 9.3 %fusion.139 = f32[256,1024]{1,0:T(8,128)S(1)} fusion(f32[1024,256]{1,0:T(8,128)} %all-gather.20.cloned.1.call-done, f32[1024,1024]{1,0:T(8,128)} %all-gather.12.cloned.1.call-done), kind=kOutput, calls=%fused_computation.203 | convolution fusion | flops 3221225472 | bytes 6291456 | tf_op jit(solution)/shard_map/dot_general | solution.py:16
  509.9 0.7 fusion.24
  510.7 0.7 fusion.23
  511.4 4.1 fusion.14
  515.7 1.7 fusion.20
  517.3 5.4 %fusion.11 = f32[1,32,1024]{2,1,0:T(8,128)} fusion(f32[32,1024]{1,0:T(8,128)S(1)} %fusion.12, f32[32,1024]{1,0:T(8,128)S(1)} %collective-permute-done.4, f32[32,1024]{1,0:T(8,128)S(1)} %fusion.24, f32[1024,1024]{1,0:T(8,128)} %all-gather.22.cloned.1.call-done, f32[1024,1024]{1,0:T(8,128)} %all-gather.12.cloned.1.call-done, s32[]{:T(128)S(6)} %select_n.93, ...), kind=kOutput, calls=%fused_computation.20 | convolution fusion | flops 402751488 | bytes 4849669 | tf_op jit(solution)/shard_map/dot_general | solution.py:16
  (129 shorter events, 17.6 us)
Async XLA Ops:
  8.0 18.1 %copy-start.13 = (s32[2,8,3]{1,0,2:T(2,128)S(1)}, s32[2,8,3]{1,0,2:T(2,128)}, u32[]{:S(2)}) copy-start(s32[2,8,3]{1,0,2:T(2,128)} %param.11) | copy-start | bytes 580
  8.0 63.6 %all-reduce.7.cloned.1.call-start = ((), (), s32[]{:S(2)}) async-start(), calls=%async_computation.1 | async-start | bytes 131072 | tf_op jit(solution)/shard_map/psum | solution.py:70
  25.5 53.1 %all-gather.10.cloned.1.call-start = ((), (), s32[]{:S(2)}) async-start(), calls=%async_computation | async-start | bytes 3244032 | tf_op jit(solution)/shard_map/all_gather | solution.py:99
  26.1 113.6 %all-reduce.9.cloned.1.call-start = ((), (), s32[]{:S(2)}) async-start(), calls=%async_computation.2 | async-start | bytes 131072 | tf_op jit(solution)/shard_map/psum | solution.py:70
  71.6 167.2 %all-gather.18.cloned.1.call-start = ((), (), s32[]{:S(2)}) async-start(), calls=%async_computation.6 | async-start | bytes 4325376 | tf_op jit(solution)/shard_map/all_gather | solution.py:78
  81.8 9.9 %copy-start.8 = (f32[2,32,1024]{2,1,0:T(8,128)S(1)}, f32[2,32,1024]{2,1,0:T(8,128)}, u32[]{:S(2)}) copy-start(f32[2,32,1024]{2,1,0:T(8,128)} %param.14) | copy-start | bytes 786436
  89.7 2.0 copy-start
  96.7 147.4 %all-gather.16.cloned.1.call-start = ((), (), s32[]{:S(2)}) async-start(), calls=%async_computation.5 | async-start | bytes 1081344 | tf_op jit(solution)/shard_map/all_gather | solution.py:126
  98.2 72.4 %copy-start.7 = (f32[8,128,128]{2,1,0:T(8,128)}, f32[8,128,128]{2,1,0:T(8,128)S(1)}, u32[]{:S(2)}) copy-start(f32[8,128,128]{2,1,0:T(8,128)S(1)} %copy.56) | copy-start | bytes 1572868
  170.7 1.9 copy-start.2
  176.4 4.9 collective-permute-start.1
  181.2 0.6 copy-start.11
  181.9 112.4 %all-reduce.11.cloned.1.call-start = ((), (), s32[]{:S(2)}) async-start(), calls=%async_computation.7 | async-start | bytes 524288 | tf_op jit(solution)/shard_map/psum | solution.py:70
  227.5 5.4 %copy-start.1 = (f32[8,8,128,128]{3,1,2,0:T(8,128)S(1)}, f32[8,8,128,128]{3,1,2,0:T(8,128)}, u32[]{:S(2)}) copy-start(f32[8,8,128,128]{3,1,2,0:T(8,128)} %copy-done) | copy-start | bytes 12582916
  243.5 51.5 %copy-start.12 = (f32[2,32]{1,0:T(2,128)S(1)}, f32[2,32]{1,0:T(2,128)}, u32[]{:S(2)}) copy-start(f32[2,32]{1,0:T(2,128)} %param.13) | copy-start | bytes 772
  243.6 88.7 %copy-start.14 = (f32[2,32]{1,0:T(2,128)S(1)}, f32[2,32]{1,0:T(2,128)}, u32[]{:S(2)}) copy-start(f32[2,32]{1,0:T(2,128)} %param.17) | copy-start | bytes 772
  245.9 48.4 %copy-start.9 = (f32[32,256]{1,0:T(8,128)}, f32[32,256]{1,0:T(8,128)S(1)}, u32[]{:S(2)}) copy-start(f32[32,256]{1,0:T(8,128)S(1)} %fusion.138) | copy-start | bytes 98308
  247.8 100.5 %copy-start.15 = (u32[256]{0:T(256)S(1)}, u32[256]{0:T(256)}, u32[]{:S(2)}) copy-start(u32[256]{0:T(256)} %constant.217) | copy-start | bytes 3076
  247.8 93.7 %all-gather.12.cloned.1.call-start = ((), (), s32[]{:S(2)}) async-start(), calls=%async_computation.3 | async-start | bytes 4325376 | tf_op jit(solution)/shard_map/all_gather | solution.py:125
  253.3 7.7 %copy-start.5 = (f32[32,1024]{1,0:T(8,128)}, f32[32,1024]{1,0:T(8,128)S(1)}, u32[]{:S(2)}) copy-start(f32[32,1024]{1,0:T(8,128)S(1)} %fusion.6) | copy-start | bytes 393220
  253.3 168.9 %copy-start.4 = (f32[1024,256]{1,0:T(8,128)S(1)}, f32[1024,256]{1,0:T(8,128)}, u32[]{:S(2)}) copy-start(f32[1024,256]{1,0:T(8,128)} %all-gather.16.cloned.1.call-done) | copy-start | bytes 3145732
  253.3 7.0 %collective-permute-start = (f32[32,1024]{1,0:T(8,128)S(1)}, f32[32,1024]{1,0:T(8,128)S(1)}, u32[]{:S(2)}, u32[]{:S(2)}) collective-permute-start(f32[32,1024]{1,0:T(8,128)S(1)} %fusion.6), channel_id=1, source_target_pairs={{32,0},{64,32},{96,64},{128,96},{160,128},{192,160},{224,192},{33,... | collective-permute-start | bytes 393224 | tf_op jit(solution)/shard_map/ppermute | solution.py:12
  260.3 0.7 copy-start.10
  261.0 165.2 %all-gather.14.cloned.1.call-start = ((), (), s32[]{:S(2)}) async-start(), calls=%async_computation.4 | async-start | bytes 4325376 | tf_op jit(solution)/shard_map/all_gather | solution.py:124
  261.7 170.3 %all-reduce.13.cloned.1.call-start = ((), (), s32[]{:S(2)}) async-start(), calls=%async_computation.8 | async-start | bytes 524288 | tf_op jit(solution)/shard_map/psum | solution.py:70
  294.3 204.4 %all-gather.20.cloned.1.call-start = ((), (), s32[]{:S(2)}) async-start(), calls=%async_computation.9 | async-start | bytes 1081344 | tf_op jit(solution)/shard_map/all_gather | solution.py:67
  295.0 222.3 %all-gather.22.cloned.1.call-start = ((), (), s32[]{:S(2)}) async-start(), calls=%async_computation.10 | async-start | bytes 4325376 | tf_op jit(solution)/shard_map/all_gather | solution.py:78
  349.7 73.1 %collective-permute-start.2 = (f32[256]{0:T(256)S(1)}, f32[256]{0:T(256)S(1)}, u32[]{:S(2)}, u32[]{:S(2)}) collective-permute-start(f32[256]{0:T(256)S(1)} %pad_maximum_fusion.5), channel_id=1, source_target_pairs={{32,0},{64,32},{96,64},{128,96},{160,128},{192,160},{224,192},{33,... | collective-permute-start | bytes 3080 | tf_op jit(solution)/shard_map/ppermute | solution.py:12
  354.4 161.3 %collective-permute-start.3 = (f32[32]{0:T(128)S(1)}, f32[32]{0:T(128)S(1)}, u32[]{:S(2)}, u32[]{:S(2)}) collective-permute-start(f32[32]{0:T(128)S(1)} %fusion.16), channel_id=1, source_target_pairs={{32,0},{64,32},{96,64},{128,96},{160,128},{192,160},{224,192},{33,... | collective-permute-start | bytes 392 | tf_op jit(solution)/shard_map/ppermute | solution.py:12
  422.8 94.5 %collective-permute-start.4 = (f32[32,1024]{1,0:T(8,128)S(1)}, f32[32,1024]{1,0:T(8,128)S(1)}, u32[]{:S(2)}, u32[]{:S(2)}) collective-permute-start(f32[32,1024]{1,0:T(8,128)S(1)} %fusion.12), channel_id=1, source_target_pairs={{32,0},{64,32},{96,64},{128,96},{160,128},{192,160},{224,192},{33,... | collective-permute-start | bytes 393224 | tf_op jit(solution)/shard_map/ppermute | solution.py:12
  507.9 3.5 copy-start.3
  507.9 3.5 copy-start.6
Sparse Core Ops, SparseCore 0:
  25.6 45.9 all-reduce.6
  74.0 65.6 all-reduce.8
  247.9 46.2 all-reduce.10
  296.5 66.9 all-reduce.12
Sparse Core Ops, SparseCore 1:
  28.6 50.0 all-gather.9
  96.7 50.6 all-gather.17
  182.0 48.5 all-gather.15
  261.0 49.6 all-gather.11
  313.8 50.9 all-gather.13
  367.4 47.3 all-gather.19
  417.2 50.9 all-gather.21
